TPU v7x, 512 devices: a whole 4x4x16 slice. The times are simulated.
512 devices in a mesh: row: 16 (over z), col: 32 (over y, x, core).
Axes of the slice: x: 4, y: 4, z: 16, core: 2. Of those that a mesh axis runs over, the one named last changes fastest.
Arguments:
- flow_state: bfloat16 [131072, 256], P(('col', 'row')), may hold values from -6 to 6
- link_state: bfloat16 [65536, 256], P(('row', 'col')), may hold values from -6 to 6
- incidence: bfloat16 [16, 32, 24, 128, 128], P('row', 'col'), may hold values from -0.29882812 to 0.29882812
- tile_flow: int32 [16, 32, 24], P('row', 'col'), may hold values from 0 to 31
- tile_link: int32 [16, 32, 24], P('row', 'col'), may hold values from 0 to 31
- tile_live: int32 [16, 32, 24], P('row', 'col'), may hold values from 0 to 1, as said below
- link_gain: float32 [256], replicated, may hold values from 0.5 to 2
- link_agg_weight: bfloat16 [256, 256], replicated, may hold values from -0.375 to 0.375
- link_self_weight: bfloat16 [256, 256], replicated, may hold values from -0.375 to 0.375
- link_out_weight: bfloat16 [256, 256], replicated, may hold values from -0.375 to 0.375
- flow_gain: float32 [256], replicated, may hold values from 0.5 to 2
- flow_agg_weight: bfloat16 [256, 256], replicated, may hold values from -0.375 to 0.375
- flow_self_weight: bfloat16 [256, 256], replicated, may hold values from -0.375 to 0.375
- flow_out_weight: bfloat16 [256, 256], replicated, may hold values from -0.375 to 0.375
Outputs:
- link_next: bfloat16 [65536, 256], P(('row', 'col'))
- flow_next: bfloat16 [131072, 256], P(('col', 'row'))
Inputs may be any that keep to these rules, and one draw needn't show every extreme that they name: `tile_live`: in every draw some group pair has all 24 slots live; the number of live slots differs from pair to pair.
All inputs are finite; a program needn't handle non-finite values.
Results may differ from a plain program's by a relative error of at most 0.018.
Values may be sent and summed in bfloat16 or wider, within the bound.
No kernel may reach another device: no remote copies, remote signals or barrier semaphores. Data moves between devices by JAX's collectives and lax.ppermute only.
A program may use at most 64 MiB of HBM per device.

v0:
```python
import jax
import jax.numpy as jnp
from jax import lax
from jax.sharding import PartitionSpec as P

H = 256
BS = 128


def state_update(totals, state, gain, agg_weight, self_weight, out_weight):
    scale = lax.rsqrt(jnp.mean(totals * totals, axis=-1, keepdims=True) + 1e-05)
    normed = (totals * scale * gain).astype(jnp.bfloat16)
    before = jnp.dot(normed, agg_weight, preferred_element_type=jnp.float32) + jnp.dot(
        state, self_weight, preferred_element_type=jnp.float32
    )
    hidden = jax.nn.silu(before).astype(jnp.bfloat16)
    return (
        state.astype(jnp.float32) + jnp.dot(hidden, out_weight, preferred_element_type=jnp.float32)
    ).astype(jnp.bfloat16)


def selector(targets, live_slots, block_count):
    select = (targets[None, :] == jnp.arange(block_count, dtype=jnp.int32)[:, None]).astype(
        jnp.float32
    )
    return select * live_slots.astype(jnp.float32)[None, :]


def on_device(
    flow_state,
    link_state,
    incidence,
    tile_flow,
    tile_link,
    tile_live,
    link_gain,
    link_agg_weight,
    link_self_weight,
    link_out_weight,
    flow_gain,
    flow_agg_weight,
    flow_self_weight,
    flow_out_weight,
):
    coefs = incidence[0, 0]
    flow_slots = tile_flow[0, 0]
    link_slots = tile_link[0, 0]
    live_slots = tile_live[0, 0]
    slot_count = coefs.shape[0]
    flow_blocks_here = flow_state.shape[0] // BS
    link_blocks_here = link_state.shape[0] // BS
    link_blocks = link_blocks_here * lax.axis_size("col")
    flow_group = lax.all_gather(flow_state, "row", axis=0, tiled=True)
    flow_blocks = flow_group.shape[0] // BS
    flow_pieces = jnp.take(flow_group.reshape(flow_blocks, BS, H), flow_slots, axis=0)
    link_terms = jnp.einsum(
        "tij,tih->tjh", coefs, flow_pieces, preferred_element_type=jnp.float32
    ).reshape(slot_count, BS * H)
    link_select = selector(link_slots, live_slots, link_blocks)
    chosen = link_select
    link_sum = lax.psum_scatter(
        jnp.dot(chosen, link_terms, precision=lax.Precision.HIGHEST).astype(jnp.bfloat16),
        "col",
        scatter_dimension=0,
        tiled=True,
    ).astype(jnp.float32)
    link_next = state_update(
        link_sum.reshape(link_blocks_here * BS, H),
        link_state,
        link_gain,
        link_agg_weight,
        link_self_weight,
        link_out_weight,
    )
    link_group = lax.all_gather(link_next, "col", axis=0, tiled=True)
    link_pieces = jnp.take(link_group.reshape(link_blocks, BS, H), link_slots, axis=0)
    flow_terms = jnp.einsum(
        "tij,tjh->tih", coefs, link_pieces, preferred_element_type=jnp.float32
    ).reshape(slot_count, BS * H)
    flow_select = selector(flow_slots, live_slots, flow_blocks)
    chosen = flow_select
    flow_sum = lax.psum_scatter(
        jnp.dot(chosen, flow_terms, precision=lax.Precision.HIGHEST).astype(jnp.bfloat16),
        "row",
        scatter_dimension=0,
        tiled=True,
    ).astype(jnp.float32)
    flow_next = state_update(
        flow_sum.reshape(flow_blocks_here * BS, H),
        flow_state,
        flow_gain,
        flow_agg_weight,
        flow_self_weight,
        flow_out_weight,
    )
    return (link_next, flow_next)


def solution(mesh):
    return jax.shard_map(
        on_device,
        mesh=mesh,
        in_specs=(
            P(("col", "row"), None),
            P(("row", "col"), None),
            P("row", "col", None, None, None),
            P("row", "col", None),
            P("row", "col", None),
            P("row", "col", None),
            P(),
            P(),
            P(),
            P(),
            P(),
            P(),
            P(),
            P(),
        ),
        out_specs=(P(("row", "col"), None), P(("col", "row"), None)),
        check_vma=False,
    )
```

profile of v0, /device:TPU:2, one launch (start us, length us, event | category | flops | bytes accessed | tf_op | source)
XLA Modules:
  0.0 468.4 jit_solution(17944627231696059716)
XLA Ops:
  7.2 0.0 copy-start
  7.2 0.0 all-gather.3.cloned.1.call-start
  7.2 0.7 all-gather.3.cloned.1.call-update
  7.9 0.0 all-reduce.5.cloned.1.call-start
  8.0 0.7 compare_select_fusion.1
  8.6 0.7 compare_and_fusion.1
  9.3 0.7 convert_bitcast_fusion
  9.9 77.7 %all-gather.3.cloned.1.call-done = bf16[4096,256]{1,0:T(8,128)(2,1)} async-done(((bf16[256,256]{1,0:T(8,128)(2,1)}), bf16[4096,256]{1,0:T(8,128)(2,1)}) %all-gather.3.cloned.1.call-update) | async-done | bytes 2097168 | tf_op jit(solution)/shard_map/all_gather | solution.py:53
  87.7 2.2 gather_fusion
  89.9 0.0 copy-done
  89.9 2.4 convolution_bitcast_fusion.1
  92.3 0.0 copy-start.6
  92.3 3.6 copy.26
  95.9 0.0 copy-done.6
  95.9 6.7 %convolution_convert_fusion.1 = bf16[32,32768]{1,0:T(8,128)(2,1)} fusion(f32[24,32768]{1,0:T(8,128)} %bitcast.40, f32[24]{0:T(128)S(1)} %convert_bitcast_fusion, s32[24]{0:T(128)S(1)} %bitcast.45), kind=kOutput, calls=%fused_computation.3 | convolution fusion | flops 303040000 | bytes 5243072 | tf_op jit(solution)/shard_map/dot_general | solution.py:62
  102.5 0.0 copy-start.2
  102.5 0.0 copy-start.4
  102.5 0.0 copy-start.8
  102.5 0.0 copy-start.9
  102.5 0.0 copy-start.12
  102.6 0.0 all-reduce.5.cloned.1.call-update
  102.6 0.0 all-gather.5.cloned.1.call-start
  102.6 1.4 dynamic-slice
  104.0 133.2 %all-reduce.5.cloned.1.call-done = bf16[32,32768]{1,0:T(8,128)(2,1)} async-done(((bf16[32,32768]{1,0:T(8,128)(2,1)}), bf16[32,32768]{1,0:T(8,128)(2,1)}) %all-reduce.5.cloned.1.call-update) | async-done | bytes 2097168
  237.2 2.1 fusion.11
  239.4 0.1 multiply_reduce_fusion.1
  239.5 0.0 copy-done.2
  239.5 0.0 copy-done.4
  239.5 0.2 fusion.15
  239.7 0.0 copy-done.8
  239.7 0.0 copy-done.9
  239.7 0.0 copy-done.12
  239.7 0.9 fusion.5
  240.7 0.0 all-gather.5.cloned.1.call-update
  240.7 0.0 all-reduce.7.cloned.1.call-start
  240.8 59.3 %all-gather.5.cloned.1.call-done = bf16[4096,256]{1,0:T(8,128)(2,1)} async-done(((bf16[128,256]{1,0:T(8,128)(2,1)}), bf16[4096,256]{1,0:T(8,128)(2,1)}) %all-gather.5.cloned.1.call-update) | async-done | bytes 2097168 | tf_op jit(solution)/shard_map/all_gather | solution.py:75
  300.1 2.2 gather_fusion.1
  302.3 2.4 convolution_bitcast_fusion
  304.7 0.0 copy-start.7
  304.7 3.6 copy.27
  308.3 0.0 copy-done.7
  308.3 6.7 %convolution_convert_fusion = bf16[32,32768]{1,0:T(8,128)(2,1)} fusion(f32[24,32768]{1,0:T(8,128)} %bitcast.39, s32[24]{0:T(128)S(1)} %bitcast.46, f32[24]{0:T(128)S(1)} %convert_bitcast_fusion), kind=kOutput, calls=%fused_computation.2 | convolution fusion | flops 303040000 | bytes 5243072 | tf_op jit(solution)/shard_map/dot_general | solution.py:83
  314.9 0.0 copy-start.1
  314.9 0.0 copy-start.5
  314.9 0.0 copy-start.3
  314.9 0.0 copy-start.10
  314.9 0.0 copy-start.11
  315.0 0.0 all-reduce.7.cloned.1.call-update
  315.0 1.4 dynamic-slice.2
  317.0 142.1 %all-reduce.7.cloned.1.call-done = bf16[32,32768]{1,0:T(8,128)(2,1)} async-done(((bf16[32,32768]{1,0:T(8,128)(2,1)}), bf16[32,32768]{1,0:T(8,128)(2,1)}) %all-reduce.7.cloned.1.call-update) | async-done | bytes 2097168
  459.0 1.1 dynamic-slice_convert_fusion
  460.2 0.2 reshape.70
  460.4 0.1 multiply_reduce_fusion
  460.6 0.0 copy-done.1
  460.6 0.0 copy-done.5
  460.6 0.2 fusion.10
  460.8 0.0 copy-done.3
  460.8 0.0 copy-done.10
  460.8 0.0 copy-done.11
  460.8 1.0 fusion.4
  (7 shorter events, 0.1 us)
Async XLA Ops:
  7.2 82.8 %copy-start = (bf16[1,1,24,128,128]{4,3,2,1,0:T(8,128)(2,1)S(1)}, bf16[1,1,24,128,128]{4,3,2,1,0:T(8,128)(2,1)}, u32[]{:S(2)}) copy-start(bf16[1,1,24,128,128]{4,3,2,1,0:T(8,128)(2,1)} %param.18) | copy-start | bytes 2359300
  7.2 80.5 %all-gather.3.cloned.1.call-start = ((), (), s32[]{:S(2)}) async-start(), calls=%async_computation | async-start | bytes 2228224 | tf_op jit(solution)/shard_map/all_gather | solution.py:53
  7.9 229.3 %all-reduce.5.cloned.1.call-start = ((), (), s32[]{:S(2)}) async-start(), calls=%async_computation.2 | async-start | bytes 4194304
  92.3 3.6 copy-start.6
  102.5 136.9 %copy-start.2 = (bf16[256,256]{1,0:T(8,128)(2,1)S(1)}, bf16[256,256]{1,0:T(8,128)(2,1)}, u32[]{:S(2)}) copy-start(bf16[256,256]{1,0:T(8,128)(2,1)} %param.23) | copy-start | bytes 393220
  102.5 137.0 %copy-start.4 = (f32[256]{0:T(256)S(1)}, f32[256]{0:T(256)}, u32[]{:S(2)}) copy-start(f32[256]{0:T(256)} %param.22) | copy-start | bytes 3076
  102.5 137.2 %copy-start.8 = (bf16[256,256]{1,0:T(8,128)(2,1)S(1)}, bf16[256,256]{1,0:T(8,128)(2,1)}, u32[]{:S(2)}) copy-start(bf16[256,256]{1,0:T(8,128)(2,1)} %param.25) | copy-start | bytes 393220
  102.5 137.2 %copy-start.9 = (bf16[256,256]{1,0:T(8,128)(2,1)S(1)}, bf16[256,256]{1,0:T(8,128)(2,1)}, u32[]{:S(2)}) copy-start(bf16[256,256]{1,0:T(8,128)(2,1)} %param.24) | copy-start | bytes 393220
  102.5 137.2 %copy-start.12 = (bf16[128,256]{1,0:T(8,128)(2,1)S(1)}, bf16[128,256]{1,0:T(8,128)(2,1)}, u32[]{:S(2)}) copy-start(bf16[128,256]{1,0:T(8,128)(2,1)} %param.17) | copy-start | bytes 196612
  102.6 197.5 %all-gather.5.cloned.1.call-start = ((), (), s32[]{:S(2)}) async-start(), calls=%async_computation.1 | async-start | bytes 2162688 | tf_op jit(solution)/shard_map/all_gather | solution.py:75
  240.7 218.3 %all-reduce.7.cloned.1.call-start = ((), (), s32[]{:S(2)}) async-start(), calls=%async_computation.3 | async-start | bytes 4194304
  304.7 3.6 copy-start.7
  314.9 145.6 %copy-start.1 = (bf16[256,256]{1,0:T(8,128)(2,1)S(1)}, bf16[256,256]{1,0:T(8,128)(2,1)}, u32[]{:S(2)}) copy-start(bf16[256,256]{1,0:T(8,128)(2,1)} %param.27) | copy-start | bytes 393220
  314.9 145.6 %copy-start.5 = (f32[256]{0:T(256)S(1)}, f32[256]{0:T(256)}, u32[]{:S(2)}) copy-start(f32[256]{0:T(256)} %param.26) | copy-start | bytes 3076
  314.9 145.9 %copy-start.3 = (bf16[256,256]{1,0:T(8,128)(2,1)S(1)}, bf16[256,256]{1,0:T(8,128)(2,1)}, u32[]{:S(2)}) copy-start(bf16[256,256]{1,0:T(8,128)(2,1)} %param.16) | copy-start | bytes 393220
  314.9 145.9 %copy-start.10 = (bf16[256,256]{1,0:T(8,128)(2,1)S(1)}, bf16[256,256]{1,0:T(8,128)(2,1)}, u32[]{:S(2)}) copy-start(bf16[256,256]{1,0:T(8,128)(2,1)} %param.29) | copy-start | bytes 393220
  314.9 145.9 %copy-start.11 = (bf16[256,256]{1,0:T(8,128)(2,1)S(1)}, bf16[256,256]{1,0:T(8,128)(2,1)}, u32[]{:S(2)}) copy-start(bf16[256,256]{1,0:T(8,128)(2,1)} %param.28) | copy-start | bytes 393220
Sparse Core Ops, SparseCore 0:
  10.1 77.5 all-gather.2
  102.7 134.4 all-reduce.4
  240.9 59.1 all-gather.4
  315.1 143.8 all-reduce.6
where the time goes:
time: 469 us; the launch traced here: 468 us
  waiting for transfers between devices  413 us (88%)
  matrix products  20.5 us (4%)
  local copies, waits for them, and re-layouts  14.7 us (3%)
  between operations  14.6 us (3%)
  other arithmetic  5.46 us (1%)
    unnamed x6, waiting for transfers between devices  276 us
    all_gather x1, waiting for transfers between devices, on_device(): flow_group = lax.all_gather(flow_state, 'row', axis=0, tiled=True)  77.7 us
    all_gather x1, waiting for transfers between devices, on_device(): link_group = lax.all_gather(link_next, 'col', axis=0, tiled=True)  59.3 us
    unnamed x30, local copies, waits for them, and re-layouts  9.94 us
  transfers between devices with their start and end apart: 4, of which 4 were waited for; matrix products, arithmetic and copies ran while one was open for 1% of the time, Pallas kernels for 0%

commit v1 on v0

--- a/solution.py
+++ b/solution.py
@@ -72,7 +72,8 @@
         link_self_weight,
         link_out_weight,
     )
-    link_group = lax.all_gather(link_next, "col", axis=0, tiled=True)
+    copies = jnp.concatenate([link_next] * lax.axis_size("col"), axis=0)
+    link_group = lax.all_to_all(copies, "col", 0, 0, tiled=True)
     link_pieces = jnp.take(link_group.reshape(link_blocks, BS, H), link_slots, axis=0)
     flow_terms = jnp.einsum(
         "tij,tjh->tih", coefs, link_pieces, preferred_element_type=jnp.float32

time: 469 us -> 445 us (0.949)
  waiting for transfers between devices: 413 us -> 381 us
  starting transfers between devices: 0.16 us -> 6.75 us
    all_gather x1 -> x0, waiting for transfers between devices: 59.3 us -> none  [on_device(): link_group = lax.all_gather(link_next, 'col', axis=0, tiled=True)]
    all_to_all x0 -> x1, waiting for transfers between devices: none -> 27.6 us  [on_device(): link_group = lax.all_to_all(copies, 'col', 0, 0, tiled=True)]
    all_to_all x0 -> x1, starting transfers between devices: none -> 6.45 us  [on_device(): link_group = lax.all_to_all(copies, 'col', 0, 0, tiled=True)]
    unnamed x30 -> x64, local copies, waits for them, and re-layouts: 9.94 us -> 11.5 us
    unnamed x6 -> x5, waiting for transfers between devices: 276 us -> 275 us
where the time goes in v1:
time: 445 us
  waiting for transfers between devices  381 us (86%)
  matrix products  21.2 us (5%)
  local copies, waits for them, and re-layouts  15.8 us (4%)
  between operations  14.9 us (3%)
  starting transfers between devices  6.75 us (2%)
  other arithmetic  5.46 us (1%)
    unnamed x5, waiting for transfers between devices  275 us
    all_gather x1, waiting for transfers between devices, on_device(): flow_group = lax.all_gather(flow_state, 'row', axis=0, tiled=True)  77.7 us
    all_to_all x1, waiting for transfers between devices, on_device(): link_group = lax.all_to_all(copies, 'col', 0, 0, tiled=True)  27.6 us
    unnamed x64, local copies, waits for them, and re-layouts  11.5 us
  transfers between devices with their start and end apart: 4, of which 4 were waited for; matrix products, arithmetic and copies ran while one was open for 1% of the time, Pallas kernels for 0%

profile of v1, /device:TPU:2, one launch (start us, length us, event | category | flops | bytes accessed | tf_op | source)
XLA Modules:
  0.0 444.9 jit_solution(8017659849406293421)
XLA Ops:
  7.2 0.0 copy-start
  7.2 0.0 all-gather.2.cloned.1.call-start
  7.2 0.7 all-gather.2.cloned.1.call-update
  7.9 0.0 all-reduce.5.cloned.1.call-start
  8.0 0.7 compare_select_fusion.1
  8.6 0.7 compare_and_fusion.1
  9.3 0.7 convert_bitcast_fusion
  9.9 77.7 %all-gather.2.cloned.1.call-done = bf16[4096,256]{1,0:T(8,128)(2,1)} async-done(((bf16[256,256]{1,0:T(8,128)(2,1)}), bf16[4096,256]{1,0:T(8,128)(2,1)}) %all-gather.2.cloned.1.call-update) | async-done | bytes 2097168 | tf_op jit(solution)/shard_map/all_gather | solution.py:53
  87.7 2.2 gather_fusion
  89.9 0.0 copy-done
  89.9 2.4 convolution_bitcast_fusion.1
  92.3 0.0 copy-start.8
  92.3 3.6 copy.26
  95.9 0.0 copy-done.8
  95.9 6.7 %convolution_convert_fusion.1 = bf16[32,32768]{1,0:T(8,128)(2,1)} fusion(f32[24,32768]{1,0:T(8,128)} %bitcast.40, f32[24]{0:T(128)S(1)} %convert_bitcast_fusion, s32[24]{0:T(128)S(1)} %bitcast.45), kind=kOutput, calls=%fused_computation.3 | convolution fusion | flops 303040000 | bytes 5243072 | tf_op jit(solution)/shard_map/dot_general | solution.py:62
  102.5 0.0 copy-start.4
  102.5 0.0 copy-start.6
  102.6 0.0 copy-start.10
  102.6 0.0 copy-start.11
  102.6 0.0 copy-start.14
  102.6 0.0 all-reduce.5.cloned.1.call-update
  102.6 1.4 dynamic-slice
  104.0 133.3 %all-reduce.5.cloned.1.call-done = bf16[32,32768]{1,0:T(8,128)(2,1)} async-done(((bf16[32,32768]{1,0:T(8,128)(2,1)}), bf16[32,32768]{1,0:T(8,128)(2,1)}) %all-reduce.5.cloned.1.call-update) | async-done | bytes 2097168
  237.3 2.1 fusion.11
  239.4 0.1 multiply_reduce_fusion.1
  239.5 0.0 copy-done.4
  239.5 0.0 copy-done.6
  239.5 0.2 fusion.15
  239.7 0.0 copy-done.10
  239.7 0.0 copy-done.11
  239.8 0.0 copy-done.14
  239.8 0.3 constant_dynamic-update-slice_fusion.31
  240.1 0.0 copy-start.1
  240.6 0.0 copy-start.2
  240.6 1.3 copy-done.2
  241.9 0.0 copy-done.1
  241.9 6.5 %all-to-all-start = ((bf16[32,128,256]{2,1,0:T(8,128)(2,1)}), bf16[32,128,256]{2,1,0:T(8,128)(2,1)S(1)}, u32[]{:S(2)}, u32[]{:S(2)}) async-start(bf16[32,128,256]{2,1,0:T(8,128)(2,1)} %bitcast.43), calls=%async_computation | async-start | bytes 4194304 | tf_op jit(solution)/shard_map/all_to_all | solution.py:76
  248.4 0.2 all-reduce.7.cloned.1.call-start
  248.6 27.6 %all-to-all-done = bf16[32,128,256]{2,1,0:T(8,128)(2,1)S(1)} async-done(((bf16[32,128,256]{2,1,0:T(8,128)(2,1)}), bf16[32,128,256]{2,1,0:T(8,128)(2,1)S(1)}, u32[]{:S(2)}, u32[]{:S(2)}) %all-to-all-start) | async-done | bytes 2097184 | tf_op jit(solution)/shard_map/all_to_all | solution.py:76
  276.2 1.8 gather_fusion.1
  278.1 3.7 convolution_bitcast_fusion
  281.8 0.0 copy-start.9
  281.8 3.6 copy.27
  285.4 0.0 copy-done.9
  285.4 6.6 %convolution_convert_fusion = bf16[32,32768]{1,0:T(8,128)(2,1)} fusion(f32[24,32768]{1,0:T(8,128)} %bitcast.39, s32[24]{0:T(128)S(1)} %bitcast.46, f32[24]{0:T(128)S(1)} %convert_bitcast_fusion), kind=kOutput, calls=%fused_computation.2 | convolution fusion | flops 303040000 | bytes 5243072 | tf_op jit(solution)/shard_map/dot_general | solution.py:84
  292.0 0.0 copy-start.3
  292.0 0.0 copy-start.7
  292.0 0.0 copy-start.5
  292.0 0.0 copy-start.12
  292.0 0.0 copy-start.13
  292.0 0.0 all-reduce.7.cloned.1.call-update
  292.1 1.4 dynamic-slice.2
  294.1 141.4 %all-reduce.7.cloned.1.call-done = bf16[32,32768]{1,0:T(8,128)(2,1)} async-done(((bf16[32,32768]{1,0:T(8,128)(2,1)}), bf16[32,32768]{1,0:T(8,128)(2,1)}) %all-reduce.7.cloned.1.call-update) | async-done | bytes 2097168
  435.5 1.1 dynamic-slice_convert_fusion
  436.7 0.2 reshape.70
  436.9 0.1 multiply_reduce_fusion
  437.0 0.0 copy-done.3
  437.0 0.0 copy-done.7
  437.0 0.2 fusion.10
  437.3 0.0 copy-done.5
  437.3 0.0 copy-done.12
  437.3 0.0 copy-done.13
  437.3 1.0 fusion.4
  (38 shorter events, 0.3 us)
Async XLA Ops:
  7.2 82.8 %copy-start = (bf16[1,1,24,128,128]{4,3,2,1,0:T(8,128)(2,1)S(1)}, bf16[1,1,24,128,128]{4,3,2,1,0:T(8,128)(2,1)}, u32[]{:S(2)}) copy-start(bf16[1,1,24,128,128]{4,3,2,1,0:T(8,128)(2,1)} %param.18) | copy-start | bytes 2359300
  7.2 80.5 %all-gather.2.cloned.1.call-start = ((), (), s32[]{:S(2)}) async-start(), calls=%async_computation.1 | async-start | bytes 2228224 | tf_op jit(solution)/shard_map/all_gather | solution.py:53
  7.9 229.3 %all-reduce.5.cloned.1.call-start = ((), (), s32[]{:S(2)}) async-start(), calls=%async_computation.2 | async-start | bytes 4194304
  92.3 3.6 copy-start.8
  102.5 137.0 %copy-start.4 = (bf16[256,256]{1,0:T(8,128)(2,1)S(1)}, bf16[256,256]{1,0:T(8,128)(2,1)}, u32[]{:S(2)}) copy-start(bf16[256,256]{1,0:T(8,128)(2,1)} %param.23) | copy-start | bytes 393220
  102.5 137.0 %copy-start.6 = (f32[256]{0:T(256)S(1)}, f32[256]{0:T(256)}, u32[]{:S(2)}) copy-start(f32[256]{0:T(256)} %param.22) | copy-start | bytes 3076
  102.6 137.2 %copy-start.10 = (bf16[256,256]{1,0:T(8,128)(2,1)S(1)}, bf16[256,256]{1,0:T(8,128)(2,1)}, u32[]{:S(2)}) copy-start(bf16[256,256]{1,0:T(8,128)(2,1)} %param.25) | copy-start | bytes 393220
  102.6 137.2 %copy-start.11 = (bf16[256,256]{1,0:T(8,128)(2,1)S(1)}, bf16[256,256]{1,0:T(8,128)(2,1)}, u32[]{:S(2)}) copy-start(bf16[256,256]{1,0:T(8,128)(2,1)} %param.24) | copy-start | bytes 393220
  102.6 137.2 %copy-start.14 = (bf16[128,256]{1,0:T(8,128)(2,1)S(1)}, bf16[128,256]{1,0:T(8,128)(2,1)}, u32[]{:S(2)}) copy-start(bf16[128,256]{1,0:T(8,128)(2,1)} %param.17) | copy-start | bytes 196612
  240.1 1.8 copy-start.1
  240.6 1.3 copy-start.2
  241.9 34.3 %all-to-all-start = ((bf16[32,128,256]{2,1,0:T(8,128)(2,1)}), bf16[32,128,256]{2,1,0:T(8,128)(2,1)S(1)}, u32[]{:S(2)}, u32[]{:S(2)}) async-start(bf16[32,128,256]{2,1,0:T(8,128)(2,1)} %bitcast.43), calls=%async_computation | async-start | bytes 4194304 | tf_op jit(solution)/shard_map/all_to_all | solution.py:76
  248.4 187.2 %all-reduce.7.cloned.1.call-start = ((), (), s32[]{:S(2)}) async-start(), calls=%async_computation.3 | async-start | bytes 4194304
  281.8 3.6 copy-start.9
  292.0 145.0 %copy-start.3 = (bf16[256,256]{1,0:T(8,128)(2,1)S(1)}, bf16[256,256]{1,0:T(8,128)(2,1)}, u32[]{:S(2)}) copy-start(bf16[256,256]{1,0:T(8,128)(2,1)} %param.27) | copy-start | bytes 393220
  292.0 145.0 %copy-start.7 = (f32[256]{0:T(256)S(1)}, f32[256]{0:T(256)}, u32[]{:S(2)}) copy-start(f32[256]{0:T(256)} %param.26) | copy-start | bytes 3076
  292.0 145.3 %copy-start.5 = (bf16[256,256]{1,0:T(8,128)(2,1)S(1)}, bf16[256,256]{1,0:T(8,128)(2,1)}, u32[]{:S(2)}) copy-start(bf16[256,256]{1,0:T(8,128)(2,1)} %param.16) | copy-start | bytes 393220
  292.0 145.3 %copy-start.12 = (bf16[256,256]{1,0:T(8,128)(2,1)S(1)}, bf16[256,256]{1,0:T(8,128)(2,1)}, u32[]{:S(2)}) copy-start(bf16[256,256]{1,0:T(8,128)(2,1)} %param.29) | copy-start | bytes 393220
  292.0 145.3 %copy-start.13 = (bf16[256,256]{1,0:T(8,128)(2,1)S(1)}, bf16[256,256]{1,0:T(8,128)(2,1)}, u32[]{:S(2)}) copy-start(bf16[256,256]{1,0:T(8,128)(2,1)} %param.28) | copy-start | bytes 393220
Sparse Core Ops, SparseCore 0:
  10.1 77.5 all-gather.1
  102.7 134.4 all-reduce.4
  292.2 143.2 all-reduce.6
